TPU v7x, 32 devices: a whole 2x2x4 slice. The times are simulated.
32 devices in a mesh: blk: 4 (over y, x), dp: 8 (over z, core).
Axes of the slice: x: 2, y: 2, z: 4, core: 2. Of those that a mesh axis runs over, the one named last changes fastest.
Arguments:
- patches: bfloat16 [4096, 64, 256], P(('blk', 'dp')), may hold values from -6 to 6
- w_mix: bfloat16 [256, 128], replicated, may hold values from -0.375 to 0.375
- w_in: bfloat16 [2048, 512], replicated, may hold values from -0.125 to 0.125
- w_out: bfloat16 [512, 128], replicated, may hold values from -0.25 to 0.25
- partner_dev: int32 [4096], P(('blk', 'dp')), may hold values from 0 to 7, as said below
- partner_row: int32 [4096], P(('blk', 'dp')), may hold values from 0 to 127, as said below
Outputs:
- loss_rows: float32 [4096], P(('blk', 'dp'))
- grad_mix: float32 [256, 128], replicated
- grad_in: float32 [2048, 512], replicated
- grad_out: float32 [512, 128], replicated
Inputs may be any that keep to these rules, and one draw needn't show every extreme that they name: Among one device's rows every dp index appears as partner_dev exactly 128/8 times. Over the rows that share a blk index, the pairs (partner_dev, partner_row) name every pair of dp index and row of a device exactly once.
All inputs are finite; a program needn't handle non-finite values.
Results may differ from a plain program's by a relative error of at most 0.012.
The roundings to bfloat16 on the way count: a program that leaves them out, or rounds other values in their place, can miss the bound.
Values may be sent and summed in bfloat16 or wider, within the bound.
No kernel may reach another device: no remote copies, remote signals or barrier semaphores. Data moves between devices by JAX's collectives and lax.ppermute only.
A program may use at most 64 MiB of HBM per device.

v0:
```python
import math
import jax
import jax.numpy as jnp
from jax import lax
from jax.sharding import PartitionSpec as P

SCALE = 10.0


def dft_table(length, freqs):
    angle_idx = jnp.arange(length, dtype=jnp.int32)
    freq_idx = jnp.arange(freqs, dtype=jnp.int32)
    phase = jnp.mod(freq_idx[None, :] * angle_idx[:, None], length).astype(jnp.float32) * (
        2.0 * math.pi / length
    )
    return jnp.concatenate([jnp.cos(phase), -jnp.sin(phase)], axis=1).astype(jnp.bfloat16)


def encode(block, w_mix, w_in, w_out):
    count, length, lanes = block.shape
    filters = w_mix.shape[1]
    freqs = w_in.shape[0] // filters
    angle_table = dft_table(length, freqs)
    spec = jnp.einsum("pac,ak->pkc", block, angle_table, preferred_element_type=jnp.float32).astype(
        jnp.bfloat16
    )
    mixed = jnp.dot(spec.reshape(-1, lanes), w_mix, preferred_element_type=jnp.float32).reshape(
        count, 2 * freqs, filters
    )
    real_part = mixed[:, :freqs]
    imag_part = mixed[:, freqs:]
    powers = real_part * real_part + imag_part * imag_part
    features = jnp.log1p(powers).reshape(count, -1)
    mean_removed = features - jnp.mean(features, axis=1, keepdims=True)
    reciprocal_scale = lax.rsqrt(
        jnp.mean(mean_removed * mean_removed, axis=1, keepdims=True) + 1e-05
    )
    normed = (mean_removed * reciprocal_scale).astype(jnp.bfloat16)
    preact = jnp.dot(normed, w_in, preferred_element_type=jnp.float32)
    hidden = jax.nn.silu(preact).astype(jnp.bfloat16)
    raw_embed = jnp.dot(hidden, w_out, preferred_element_type=jnp.float32)
    norms = jnp.sqrt(jnp.sum(raw_embed * raw_embed, axis=1, keepdims=True) + 1e-06)
    unit32 = raw_embed / norms
    saved = (
        spec,
        real_part,
        imag_part,
        powers,
        mean_removed,
        reciprocal_scale,
        normed,
        preact,
        hidden,
        unit32,
        norms,
    )
    return (unit32.astype(jnp.bfloat16), saved)


def back_upper(grad_units, saved, w_in, w_out):
    (
        spec,
        real_part,
        imag_part,
        powers,
        mean_removed,
        reciprocal_scale,
        normed,
        preact,
        hidden,
        unit32,
        norms,
    ) = saved
    grad_raw = (
        (grad_units - unit32 * jnp.sum(unit32 * grad_units, axis=1, keepdims=True)) / norms
    ).astype(jnp.bfloat16)
    g_out = jnp.dot(hidden.T, grad_raw, preferred_element_type=jnp.float32)
    grad_hid = jnp.dot(grad_raw, w_out.T, preferred_element_type=jnp.float32)
    sigm = jax.nn.sigmoid(preact)
    grad_pre = (grad_hid * sigm * (1.0 + preact * (1.0 - sigm))).astype(jnp.bfloat16)
    g_in = jnp.dot(normed.T, grad_pre, preferred_element_type=jnp.float32)
    norm_gradient = jnp.dot(grad_pre, w_in.T, preferred_element_type=jnp.float32)
    return (g_in, g_out, norm_gradient)


def back_lower(norm_gradient, saved):
    (
        spec,
        real_part,
        imag_part,
        powers,
        mean_removed,
        reciprocal_scale,
        normed,
        preact,
        hidden,
        unit32,
        norms,
    ) = saved
    lanes = spec.shape[2]
    normalized_input = mean_removed * reciprocal_scale
    feature_gradient = reciprocal_scale * (
        norm_gradient
        - jnp.mean(norm_gradient, axis=1, keepdims=True)
        - normalized_input * jnp.mean(norm_gradient * normalized_input, axis=1, keepdims=True)
    )
    grad_pow = feature_gradient.reshape(powers.shape) / (1.0 + powers)
    grad_mixed = jnp.concatenate(
        [2.0 * real_part * grad_pow, 2.0 * imag_part * grad_pow], axis=1
    ).astype(jnp.bfloat16)
    return jnp.dot(
        spec.reshape(-1, lanes).T,
        grad_mixed.reshape(-1, grad_mixed.shape[2]),
        preferred_element_type=jnp.float32,
    )


def negative_part(units, piece, row_ids):
    scores = SCALE * jnp.dot(units, piece.T, preferred_element_type=jnp.float32)
    column = jnp.arange(piece.shape[0], dtype=jnp.int32)
    expo = jnp.where(column[None, :] == row_ids[:, None], jnp.float32(0.0), jnp.exp(scores))
    return (
        jnp.sum(expo, axis=1),
        jnp.dot(expo.astype(jnp.bfloat16), piece, preferred_element_type=jnp.float32),
    )


def key_part(units, piece, tot_piece, row_ids):
    scores = SCALE * jnp.dot(piece, units.T, preferred_element_type=jnp.float32)
    column = jnp.arange(piece.shape[0], dtype=jnp.int32)
    expo = jnp.where(column[:, None] == row_ids[None, :], jnp.float32(0.0), jnp.exp(scores))
    weights = (expo / tot_piece[:, None]).astype(jnp.bfloat16)
    return jnp.dot(weights.T, piece, preferred_element_type=jnp.float32)


def on_device(patches, w_mix, w_in, w_out, partner_dev, partner_row):
    count = patches.shape[0]
    embed = w_out.shape[1]
    units, saved = encode(patches, w_mix, w_in, w_out)
    peers = lax.axis_size("dp")
    per_peer = count // peers
    sorted_positions = jnp.argsort(partner_dev, stable=True)
    inverse = jnp.argsort(sorted_positions, stable=True)
    wanted = partner_row[sorted_positions].reshape(peers, per_peer)
    asked = lax.all_to_all(wanted, "dp", split_axis=0, concat_axis=0, tiled=True)
    picked = units[asked]
    returned_rows = lax.all_to_all(picked, "dp", split_axis=0, concat_axis=0, tiled=True)
    positive = returned_rows.reshape(count, embed)[inverse]
    spos = SCALE * jnp.sum(units.astype(jnp.float32) * positive.astype(jnp.float32), axis=1)
    row_ids = lax.axis_index("blk") * count + jnp.arange(count, dtype=jnp.int32)
    zpart, npart = negative_part(units, lax.all_gather(units, "blk", axis=0, tiled=True), row_ids)
    totals = jnp.exp(spos) + zpart
    all_totals = lax.all_gather(totals, "blk", axis=0, tiled=True)
    keyterm = key_part(units, lax.all_gather(units, "blk", axis=0, tiled=True), all_totals, row_ids)
    loss_rows = jnp.log(totals) - spos
    coef = SCALE / count
    ppos = jnp.exp(spos) / totals
    partner_grad = coef * (ppos - 1.0)[:, None] * units.astype(jnp.float32)
    outgoing = partner_grad[sorted_positions].reshape(peers, per_peer, embed)
    incoming = lax.all_to_all(outgoing, "dp", split_axis=0, concat_axis=0, tiled=True)
    from_partner = (
        jnp.zeros((count, embed), jnp.float32)
        .at[asked.reshape(-1)]
        .add(incoming.reshape(-1, embed))
    )
    grad_units = (
        coef * ((ppos - 1.0)[:, None] * positive.astype(jnp.float32) + npart / totals[:, None])
        + coef * keyterm
        + from_partner
    )
    g_in, g_out, norm_gradient = back_upper(grad_units, saved, w_in, w_out)
    g_mix = back_lower(norm_gradient, saved)
    g_mix, g_in, g_out = lax.psum((g_mix, g_in, g_out), ("blk", "dp"))
    return (loss_rows, g_mix, g_in, g_out)


def solution(mesh):
    placed = (P(("blk", "dp"), None, None), P(), P(), P(), P(("blk", "dp")), P(("blk", "dp")))
    return jax.shard_map(
        on_device,
        mesh=mesh,
        in_specs=placed,
        out_specs=(P(("blk", "dp")), P(), P(), P()),
        check_vma=False,
    )
```

profile of v0, /device:TPU:0, one launch (start us, length us, event | category | flops | bytes accessed | tf_op | source)
XLA Modules:
  0.0 252.2 jit_solution(4154058484988354202)
XLA Ops:
  7.2 3.3 %sort.31 = (s32[128]{0:T(128)}, s32[128]{0:T(128)S(1)}) sort(s32[128]{0:T(128)} %param.10, s32[128]{0:T(128)S(1)} %iota.30), dimensions={0}, to_apply=%region_3.4 | sort | flops 896 | bytes 2048 | tf_op jit(solution)/shard_map/jit(argsort)/sort | solution.py:142
  10.5 1.6 gather_fusion
  12.8 6.4 %all-to-all-start = ((s32[8,1,16]{2,1,0:T(1,128)}), s32[8,1,16]{2,1,0:T(1,128)S(1)}, u32[]{:S(2)}, u32[]{:S(2)}) async-start(s32[8,1,16]{2,1,0:T(1,128)} %bitcast.4), calls=%async_computation | async-start | bytes 8192 | tf_op jit(solution)/shard_map/all_to_all | solution.py:145
  19.3 2.5 %sort.32 = (s32[128]{0:T(128)}, s32[128]{0:T(128)S(1)}) sort(s32[128]{0:T(128)S(1)} %get-tuple-element.6, s32[128]{0:T(128)S(1)} %iota.31), dimensions={0}, to_apply=%region_4.5 | sort | flops 896 | bytes 2048 | tf_op jit(solution)/shard_map/jit(argsort)/sort | solution.py:143
  21.8 2.9 %convert_bitcast_fusion = bf16[128,32,256]{2,1,0:T(8,128)(2,1)S(1)} fusion(bf16[128,64,256]{2,1,0:T(8,128)(2,1)} %param.6, bf16[64,16]{0,1:T(8,128)(2,1)S(1)} %get-tuple-element.27, bf16[64,16]{0,1:T(8,128)(2,1)S(1)} %get-tuple-element.28), kind=kOutput, calls=%fused_computation.7 | convolution fusion | flops 135274496 | bytes 6295552 | tf_op jit(solution)/shard_map/pac,ak->pkc/dot_general | solution.py:24
  24.8 2.5 fusion
  28.9 1.6 copy.38
  30.5 1.2 multiply_convert_fusion.2
  32.0 8.5 %all_gather.7 = bf16[512,128]{0,1:T(8,128)(2,1)S(1)} all-gather(bf16[128,128]{0,1:T(8,128)(2,1)S(1)} %fusion.35), channel_id=1, replica_groups=mesh['blk'=4,'dp'=8] {'blk'}, dimensions={0}, use_global_device_ids=true | all-gather | bytes 163840 | tf_op jit(solution)/shard_map/all_gather | solution.py:151
  42.9 1.3 gather_fusion.1
  44.2 5.1 %all-to-all-start.1 = ((bf16[8,16,128]{2,1,0:T(8,128)(2,1)}), bf16[8,16,128]{2,1,0:T(8,128)(2,1)S(1)}, u32[]{:S(2)}, u32[]{:S(2)}) async-start(bf16[8,16,128]{2,1,0:T(8,128)(2,1)} %bitcast.6), calls=%async_computation.1 | async-start | bytes 65536 | tf_op jit(solution)/shard_map/all_to_all | solution.py:147
  49.9 5.2 %all-to-all-done.1 = bf16[8,16,128]{2,1,0:T(8,128)(2,1)S(1)} async-done(((bf16[8,16,128]{2,1,0:T(8,128)(2,1)}), bf16[8,16,128]{2,1,0:T(8,128)(2,1)S(1)}, u32[]{:S(2)}, u32[]{:S(2)}) %all-to-all-start.1) | async-done | bytes 32800 | tf_op jit(solution)/shard_map/all_to_all | solution.py:147
  56.4 8.5 %all-gather = f32[4,1,128]{2,1,0:T(1,128)} all-gather(f32[1,1,128]{2,1,0:T(1,128)S(1)} %bitcast.47), channel_id=1, replica_groups=mesh['blk'=4,'dp'=8] {'blk'}, dimensions={0}, use_global_device_ids=true | all-gather | bytes 2560 | tf_op jit(solution)/shard_map/all_gather | solution.py:153
  65.1 1.2 gather_fusion.3
  66.3 3.5 %all-to-all-start.2 = ((f32[8,16,128]{2,1,0:T(8,128)}), f32[8,16,128]{2,1,0:T(8,128)S(1)}, u32[]{:S(2)}, u32[]{:S(2)}) async-start(f32[8,16,128]{2,1,0:T(8,128)} %bitcast.11), calls=%async_computation.2 | async-start | bytes 131072 | tf_op jit(solution)/shard_map/all_to_all | solution.py:160
  69.9 1.2 fusion.13
  71.0 2.0 fusion.12
  73.1 0.9 copy.45
  74.0 1.7 all-to-all-done.2
  75.7 1.5 scatter_fusion
  77.3 1.8 fusion.44
  79.1 1.2 fusion.9
  80.3 0.9 fusion.40
  81.2 2.8 %fusion.36 = f32[2048,512]{1,0:T(8,128)} fusion(bf16[128,512]{1,0:T(8,128)(2,1)S(1)} %fusion.9, f32[128,2048]{1,0:T(8,128)S(1)} %copy.38, f32[128]{0:T(128)S(1)} %add_rsqrt_fusion, f32[128]{0:T(128)S(1)} %broadcast_multiply_fusion.4), kind=kOutput, calls=%fused_computation.91 | convolution fusion | flops 269221888 | bytes 5374976 | tf_op jit(solution)/shard_map/dot_general | solution.py:81
  84.1 1.4 subtract_multiply_fusion
  85.5 1.5 copy.48
  87.0 2.0 multiply_convert_fusion.1
  89.1 1.7 copy.49
  90.8 3.3 %convolution_bitcast_fusion = f32[256,128]{1,0:T(8,128)} fusion(bf16[128,32,256]{2,1,0:T(8,128)(2,1)} %copy-done.3, bf16[128,32,128]{2,1,0:T(8,128)(2,1)} %copy.49), kind=kOutput, calls=%fused_computation.19 | convolution fusion | flops 268435456 | bytes 3276800 | tf_op jit(solution)/shard_map/dot_general | solution.py:111
  95.3 143.1 %all-reduce.3.cloned.1.call-done = (f32[256,128]{1,0:T(8,128)}, f32[2048,512]{1,0:T(8,128)}, f32[512,128]{1,0:T(8,128)}) async-done(((f32[256,128]{1,0:T(8,128)}, f32[2048,512]{1,0:T(8,128)}, f32[512,128]{1,0:T(8,128)}), (f32[256,128]{1,0:T(8,128)}, f32[2048,512]{1,0:T(8,128)}, f32[512,128]{1,0:T(8,128)})) %all-reduce.3.cloned.1.call-update) | async-done | bytes 4587536 | tf_op jit(solution)/shard_map/psum | solution.py:173
  238.4 1.6 copy.60
  239.9 4.7 %copy.61 = f32[2048,512]{1,0:T(8,128)} copy(f32[2048,512]{1,0:T(8,128)} %get-tuple-element.33) | data formatting | bytes 8388608
  (71 shorter events, 9.3 us)
Async XLA Ops:
  7.2 23.3 %copy-start = (bf16[2048,512]{1,0:T(8,128)(2,1)S(1)}, bf16[2048,512]{1,0:T(8,128)(2,1)}, u32[]{:S(2)}) copy-start(bf16[2048,512]{1,0:T(8,128)(2,1)} %param.8) | copy-start | bytes 6291460
  12.8 28.7 %all-to-all-start = ((s32[8,1,16]{2,1,0:T(1,128)}), s32[8,1,16]{2,1,0:T(1,128)S(1)}, u32[]{:S(2)}, u32[]{:S(2)}) async-start(s32[8,1,16]{2,1,0:T(1,128)} %bitcast.4), calls=%async_computation | async-start | bytes 8192 | tf_op jit(solution)/shard_map/all_to_all | solution.py:145
  19.2 21.2 %copy-start.14 = (s32[128]{0:T(128)}, s32[128]{0:T(128)S(1)}, u32[]{:S(2)}) copy-start(s32[128]{0:T(128)S(1)} %iota_add_fusion) | copy-start | bytes 1540
  21.8 2.9 %copy-start.8 = (bf16[256,128]{1,0:T(8,128)(2,1)S(1)}, bf16[256,128]{1,0:T(8,128)(2,1)}, u32[]{:S(2)}) copy-start(bf16[256,128]{1,0:T(8,128)(2,1)} %param.7) | copy-start | bytes 196612
  24.7 2.5 %copy-start.3 = (bf16[128,32,256]{2,1,0:T(8,128)(2,1)}, bf16[128,32,256]{2,1,0:T(8,128)(2,1)S(1)}, u32[]{:S(2)}) copy-start(bf16[128,32,256]{2,1,0:T(8,128)(2,1)S(1)} %convert_bitcast_fusion) | copy-start | bytes 6291460
  27.3 1.3 copy-start.1
  27.8 1.2 copy-start.2
  30.5 1.2 copy-start.5
  31.7 9.7 %copy-start.6 = (bf16[128,512]{1,0:T(8,128)(2,1)}, bf16[128,512]{1,0:T(8,128)(2,1)S(1)}, u32[]{:S(2)}) copy-start(bf16[128,512]{1,0:T(8,128)(2,1)S(1)} %get-tuple-element.20) | copy-start | bytes 393220
  40.5 0.9 copy-start.7
  44.2 10.8 %all-to-all-start.1 = ((bf16[8,16,128]{2,1,0:T(8,128)(2,1)}), bf16[8,16,128]{2,1,0:T(8,128)(2,1)S(1)}, u32[]{:S(2)}, u32[]{:S(2)}) async-start(bf16[8,16,128]{2,1,0:T(8,128)(2,1)} %bitcast.6), calls=%async_computation.1 | async-start | bytes 65536 | tf_op jit(solution)/shard_map/all_to_all | solution.py:147
  55.9 9.1 %copy-start.9 = (f32[128]{0:T(128)}, f32[128]{0:T(128)S(1)}, u32[]{:S(2)}) copy-start(f32[128]{0:T(128)S(1)} %fusion.21) | copy-start | bytes 1540
  56.4 8.6 %copy-start.11 = (f32[128]{0:T(128)}, f32[128]{0:T(128)S(1)}, u32[]{:S(2)}) copy-start(f32[128]{0:T(128)S(1)} %get-tuple-element.15) | copy-start | bytes 1540
  66.3 9.3 %copy-start.13 = (s32[128]{0:T(128)S(1)}, s32[128]{0:T(128)}, u32[]{:S(2)}) copy-start(s32[128]{0:T(128)} %fusion.31) | copy-start | bytes 1540
  66.3 9.3 %all-to-all-start.2 = ((f32[8,16,128]{2,1,0:T(8,128)}), f32[8,16,128]{2,1,0:T(8,128)S(1)}, u32[]{:S(2)}, u32[]{:S(2)}) async-start(f32[8,16,128]{2,1,0:T(8,128)} %bitcast.11), calls=%async_computation.2 | async-start | bytes 131072 | tf_op jit(solution)/shard_map/all_to_all | solution.py:160
  69.8 168.5 %all-reduce.3.cloned.1.call-start = ((), (), s32[]{:S(2)}) async-start(), calls=%async_computation.3 | async-start | bytes 9175040 | tf_op jit(solution)/shard_map/psum | solution.py:173
  94.1 0.7 copy-start.10
  94.1 0.7 copy-start.12
  239.9 4.7 %copy-start.4 = (f32[512,128]{1,0:T(8,128)S(1)}, f32[512,128]{1,0:T(8,128)}, u32[]{:S(2)}) copy-start(f32[512,128]{1,0:T(8,128)} %get-tuple-element.34) | copy-start | bytes 786436
Sparse Core Ops, SparseCore 0:
  94.2 144.0 all-reduce.2
where the time goes:
time: 253 us; the launch traced here: 252 us
  waiting for transfers between devices  150 us (59%)
  matrix products  21 us (8%)
  local copies, waits for them, and re-layouts  20.8 us (8%)
  blocking collectives  17 us (7%)
  starting transfers between devices  15 us (6%)
  between operations  14.3 us (6%)
  other arithmetic  14.1 us (6%)
    psum x1, waiting for transfers between devices, on_device(): g_mix, g_in, g_out = lax.psum((g_mix, g_in, g_out), ('blk', 'dp'))  143 us
    all_gather x1, blocking collectives, on_device(): all_totals = lax.all_gather(totals, 'blk', axis=0, tiled=True)  8.55 us
    unnamed x33, local copies, waits for them, and re-layouts  8.52 us
    all_gather x1, blocking collectives, on_device(): lax.all_gather(units, 'blk', axis=0, tiled=True)  8.46 us
    all_to_all x1, starting transfers between devices, on_device(): lax.all_to_all(wanted, 'dp', split_axis=0, concat_axis=0, tiled=True)  6.35 us
    all_to_all x1, waiting for transfers between devices, on_device(): lax.all_to_all(picked, 'dp', split_axis=0, concat_axis=0, tiled=True)  5.16 us
    all_to_all x1, starting transfers between devices, on_device(): lax.all_to_all(picked, 'dp', split_axis=0, concat_axis=0, tiled=True)  5.09 us
  transfers between devices with their start and end apart: 4, of which 3 were waited for; matrix products, arithmetic and copies ran while one was open for 7% of the time, Pallas kernels for 0%

commit v1 on v0

--- a/solution.py
+++ b/solution.py
@@ -1,3 +1,4 @@
+import functools
 import math
 import jax
 import jax.numpy as jnp
@@ -5,6 +6,15 @@
 from jax.sharding import PartitionSpec as P
 
 SCALE = 10.0
+
+
+def move_core_in(block_in, which_axis, axis_name):
+    for dev_i in (which_axis, axis_name):
+        block_in = lax.psum(block_in, axis_name=dev_i)
+    return block_in
+
+
+point_view = functools.partial(move_core_in, which_axis="dp", axis_name="blk")
 
 
 def dft_table(length, freqs):
@@ -170,7 +180,7 @@
     )
     g_in, g_out, norm_gradient = back_upper(grad_units, saved, w_in, w_out)
     g_mix = back_lower(norm_gradient, saved)
-    g_mix, g_in, g_out = lax.psum((g_mix, g_in, g_out), ("blk", "dp"))
+    g_mix, g_in, g_out = point_view((g_mix, g_in, g_out))
     return (loss_rows, g_mix, g_in, g_out)
 
 

time: 253 us -> 325 us (1.28)
  waiting for transfers between devices: 150 us -> 223 us
    psum x1 -> x2, waiting for transfers between devices: 143 us -> 216 us  [move_core_in(): block_in = lax.psum(block_in, axis_name=dev_i)]
  transfers between devices with their start and end apart: 4 -> 5, of which waited for: 3 -> 4; matrix products, arithmetic and copies ran while one was open for 7% -> 6% of each run, Pallas kernels for 0% -> 0%
where the time goes in v1:
time: 325 us
  waiting for transfers between devices  223 us (69%)
  matrix products  21 us (6%)
  local copies, waits for them, and re-layouts  20.8 us (6%)
  blocking collectives  17 us (5%)
  starting transfers between devices  15 us (5%)
  between operations  14.3 us (4%)
  other arithmetic  14.1 us (4%)
    psum x2, waiting for transfers between devices, move_core_in(): block_in = lax.psum(block_in, axis_name=dev_i)  216 us
    all_gather x1, blocking collectives, on_device(): all_totals = lax.all_gather(totals, 'blk', axis=0, tiled=True)  8.54 us
    unnamed x33, local copies, waits for them, and re-layouts  8.49 us
    all_gather x1, blocking collectives, on_device(): lax.all_gather(units, 'blk', axis=0, tiled=True)  8.46 us
  transfers between devices with their start and end apart: 5, of which 4 were waited for; matrix products, arithmetic and copies ran while one was open for 6% of the time, Pallas kernels for 0%

profile of v1, /device:TPU:0, one launch (start us, length us, event | category | flops | bytes accessed | tf_op | source)
XLA Modules:
  0.0 324.8 jit_solution(1809138240115954826)
XLA Ops:
  7.2 3.3 %sort.31 = (s32[128]{0:T(128)}, s32[128]{0:T(128)S(1)}) sort(s32[128]{0:T(128)} %param.10, s32[128]{0:T(128)S(1)} %iota.30), dimensions={0}, to_apply=%region_3.4 | sort | flops 896 | bytes 2048 | tf_op jit(solution)/shard_map/jit(argsort)/sort | solution.py:152
  10.5 1.6 gather_fusion
  12.8 6.4 %all-to-all-start = ((s32[8,1,16]{2,1,0:T(1,128)}), s32[8,1,16]{2,1,0:T(1,128)S(1)}, u32[]{:S(2)}, u32[]{:S(2)}) async-start(s32[8,1,16]{2,1,0:T(1,128)} %bitcast.4), calls=%async_computation | async-start | bytes 8192 | tf_op jit(solution)/shard_map/all_to_all | solution.py:155
  19.3 2.5 sort.32
  21.8 2.9 convert_bitcast_fusion
  24.8 2.5 fusion
  28.9 1.6 copy.38
  30.5 1.2 multiply_convert_fusion.2
  32.0 8.5 %all_gather.7 = bf16[512,128]{0,1:T(8,128)(2,1)S(1)} all-gather(bf16[128,128]{0,1:T(8,128)(2,1)S(1)} %fusion.35), channel_id=1, replica_groups=mesh['blk'=4,'dp'=8] {'blk'}, dimensions={0}, use_global_device_ids=true | all-gather | bytes 163840 | tf_op jit(solution)/shard_map/all_gather | solution.py:161
  42.9 1.3 gather_fusion.1
  44.2 5.1 %all-to-all-start.1 = ((bf16[8,16,128]{2,1,0:T(8,128)(2,1)}), bf16[8,16,128]{2,1,0:T(8,128)(2,1)S(1)}, u32[]{:S(2)}, u32[]{:S(2)}) async-start(bf16[8,16,128]{2,1,0:T(8,128)(2,1)} %bitcast.6), calls=%async_computation.1 | async-start | bytes 65536 | tf_op jit(solution)/shard_map/all_to_all | solution.py:157
  49.9 5.2 %all-to-all-done.1 = bf16[8,16,128]{2,1,0:T(8,128)(2,1)S(1)} async-done(((bf16[8,16,128]{2,1,0:T(8,128)(2,1)}), bf16[8,16,128]{2,1,0:T(8,128)(2,1)S(1)}, u32[]{:S(2)}, u32[]{:S(2)}) %all-to-all-start.1) | async-done | bytes 32800 | tf_op jit(solution)/shard_map/all_to_all | solution.py:157
  56.4 8.5 %all-gather = f32[4,1,128]{2,1,0:T(1,128)} all-gather(f32[1,1,128]{2,1,0:T(1,128)S(1)} %bitcast.47), channel_id=1, replica_groups=mesh['blk'=4,'dp'=8] {'blk'}, dimensions={0}, use_global_device_ids=true | all-gather | bytes 2560 | tf_op jit(solution)/shard_map/all_gather | solution.py:163
  65.1 1.2 gather_fusion.3
  66.3 3.5 %all-to-all-start.2 = ((f32[8,16,128]{2,1,0:T(8,128)}), f32[8,16,128]{2,1,0:T(8,128)S(1)}, u32[]{:S(2)}, u32[]{:S(2)}) async-start(f32[8,16,128]{2,1,0:T(8,128)} %bitcast.11), calls=%async_computation.2 | async-start | bytes 131072 | tf_op jit(solution)/shard_map/all_to_all | solution.py:170
  69.9 1.2 fusion.13
  71.0 2.0 fusion.12
  73.1 0.9 copy.45
  74.0 1.7 all-to-all-done.2
  75.7 1.5 scatter_fusion
  77.3 1.8 fusion.44
  79.1 1.2 fusion.9
  81.2 2.8 fusion.36
  84.1 1.4 subtract_multiply_fusion
  85.5 1.5 copy.48
  87.1 2.0 multiply_convert_fusion.1
  89.1 1.7 copy.49
  90.8 3.3 %convolution_bitcast_fusion = f32[256,128]{1,0:T(8,128)} fusion(bf16[128,32,256]{2,1,0:T(8,128)(2,1)} %copy-done.3, bf16[128,32,128]{2,1,0:T(8,128)(2,1)} %copy.49), kind=kOutput, calls=%fused_computation.19 | convolution fusion | flops 268435456 | bytes 3276800 | tf_op jit(solution)/shard_map/dot_general | solution.py:121
  94.2 102.8 %all-reduce.5.cloned.1.call-done = (f32[256,128]{1,0:T(8,128)}, f32[2048,512]{1,0:T(8,128)}, f32[512,128]{1,0:T(8,128)}) async-done(((f32[256,128]{1,0:T(8,128)}, f32[2048,512]{1,0:T(8,128)}, f32[512,128]{1,0:T(8,128)}), (f32[256,128]{1,0:T(8,128)}, f32[2048,512]{1,0:T(8,128)}, f32[512,128]{1,0:T(8,128)})) %all-reduce.5.cloned.1.call-update) | async-done | bytes 4587536 | tf_op jit(solution)/shard_map/psum | solution.py:13
  198.1 112.9 %all-reduce.7.cloned.1.call-done = (f32[256,128]{1,0:T(8,128)}, f32[2048,512]{1,0:T(8,128)}, f32[512,128]{1,0:T(8,128)}) async-done(((f32[256,128]{1,0:T(8,128)}, f32[2048,512]{1,0:T(8,128)}, f32[512,128]{1,0:T(8,128)}), (f32[256,128]{1,0:T(8,128)}, f32[2048,512]{1,0:T(8,128)}, f32[512,128]{1,0:T(8,128)})) %all-reduce.7.cloned.1.call-update) | async-done | bytes 4587536 | tf_op jit(solution)/shard_map/psum | solution.py:13
  311.0 1.6 copy.63
  312.6 4.7 %copy.64 = f32[2048,512]{1,0:T(8,128)} copy(f32[2048,512]{1,0:T(8,128)} %get-tuple-element.36) | data formatting | bytes 8388608
  (74 shorter events, 10.3 us)
Async XLA Ops:
  7.2 23.3 %copy-start = (bf16[2048,512]{1,0:T(8,128)(2,1)S(1)}, bf16[2048,512]{1,0:T(8,128)(2,1)}, u32[]{:S(2)}) copy-start(bf16[2048,512]{1,0:T(8,128)(2,1)} %param.8) | copy-start | bytes 6291460
  12.8 28.7 %all-to-all-start = ((s32[8,1,16]{2,1,0:T(1,128)}), s32[8,1,16]{2,1,0:T(1,128)S(1)}, u32[]{:S(2)}, u32[]{:S(2)}) async-start(s32[8,1,16]{2,1,0:T(1,128)} %bitcast.4), calls=%async_computation | async-start | bytes 8192 | tf_op jit(solution)/shard_map/all_to_all | solution.py:155
  19.2 21.2 %copy-start.14 = (s32[128]{0:T(128)}, s32[128]{0:T(128)S(1)}, u32[]{:S(2)}) copy-start(s32[128]{0:T(128)S(1)} %iota_add_fusion) | copy-start | bytes 1540
  21.8 2.9 copy-start.8
  24.7 2.5 copy-start.3
  27.3 1.3 copy-start.1
  27.8 1.2 copy-start.2
  30.5 1.2 copy-start.5
  31.7 9.7 %copy-start.6 = (bf16[128,512]{1,0:T(8,128)(2,1)}, bf16[128,512]{1,0:T(8,128)(2,1)S(1)}, u32[]{:S(2)}) copy-start(bf16[128,512]{1,0:T(8,128)(2,1)S(1)} %get-tuple-element.23) | copy-start | bytes 393220
  40.5 0.9 copy-start.7
  44.2 10.8 %all-to-all-start.1 = ((bf16[8,16,128]{2,1,0:T(8,128)(2,1)}), bf16[8,16,128]{2,1,0:T(8,128)(2,1)S(1)}, u32[]{:S(2)}, u32[]{:S(2)}) async-start(bf16[8,16,128]{2,1,0:T(8,128)(2,1)} %bitcast.6), calls=%async_computation.1 | async-start | bytes 65536 | tf_op jit(solution)/shard_map/all_to_all | solution.py:157
  55.9 9.1 %copy-start.9 = (f32[128]{0:T(128)}, f32[128]{0:T(128)S(1)}, u32[]{:S(2)}) copy-start(f32[128]{0:T(128)S(1)} %fusion.21) | copy-start | bytes 1540
  56.4 8.6 %copy-start.11 = (f32[128]{0:T(128)}, f32[128]{0:T(128)S(1)}, u32[]{:S(2)}) copy-start(f32[128]{0:T(128)S(1)} %get-tuple-element.18) | copy-start | bytes 1540
  66.3 9.3 %copy-start.13 = (s32[128]{0:T(128)S(1)}, s32[128]{0:T(128)}, u32[]{:S(2)}) copy-start(s32[128]{0:T(128)} %fusion.31) | copy-start | bytes 1540
  66.3 9.3 %all-to-all-start.2 = ((f32[8,16,128]{2,1,0:T(8,128)}), f32[8,16,128]{2,1,0:T(8,128)S(1)}, u32[]{:S(2)}, u32[]{:S(2)}) async-start(f32[8,16,128]{2,1,0:T(8,128)} %bitcast.11), calls=%async_computation.2 | async-start | bytes 131072 | tf_op jit(solution)/shard_map/all_to_all | solution.py:170
  69.8 127.1 %all-reduce.5.cloned.1.call-start = ((), (), s32[]{:S(2)}) async-start(), calls=%async_computation.3 | async-start | bytes 9175040 | tf_op jit(solution)/shard_map/psum | solution.py:13
  94.1 216.9 %all-reduce.7.cloned.1.call-start = ((), (), s32[]{:S(2)}) async-start(), calls=%async_computation.4 | async-start | bytes 9175040 | tf_op jit(solution)/shard_map/psum | solution.py:13
  197.0 0.6 copy-start.10
  197.0 0.6 copy-start.12
  312.6 4.7 %copy-start.4 = (f32[512,128]{1,0:T(8,128)S(1)}, f32[512,128]{1,0:T(8,128)}, u32[]{:S(2)}) copy-start(f32[512,128]{1,0:T(8,128)} %get-tuple-element.37) | copy-start | bytes 786436
Sparse Core Ops, SparseCore 0:
  94.3 102.6 all-reduce.4
  200.8 110.1 all-reduce.6
